TPU v7x, 128 devices: a whole 4x4x4 slice. The times are simulated.
128 devices in a mesh: group: 8 (over x, core), sub: 16 (over z, y).
Axes of the slice: x: 4, y: 4, z: 4, core: 2. Of those that a mesh axis runs over, the one named last changes fastest.
Arguments:
- schur: bfloat16 [8, 16, 1024, 1024], P('group', 'sub'), as said below
- local_inverse: bfloat16 [8, 16, 1024, 1024], P('group', 'sub'), as said below
- rhs_parts: bfloat16 [8, 16, 1024, 128], P('group', 'sub'), may hold values from -6 to 6
- basis: bfloat16 [8, 16, 32, 1024], P('group', 'sub'), may hold values from -0.1875 to 0.1875
- coarse_map: int32 [8, 16, 32], P('group', 'sub'), may hold values from 0 to 1023
- coarse_inverse: bfloat16 [8, 1024, 1024], P('group', 'sub'), as said below
- shared_rows: int32 [8, 16, 2, 4, 256], P('group', 'sub'), may hold values from 0 to 1023, as said below
- shared_counts: int32 [8, 16, 4], P('group', 'sub'), may hold values from 0 to 256, as said below
Outputs:
- solution: float32 [8, 16, 1024, 128], P('group', 'sub')
- residual: float32 [8, 16, 1024, 128], P('group', 'sub')
Inputs may be any that keep to these rules, and one draw needn't show every extreme that they name: `schur`: each subdomain matrix is symmetric positive definite. `local_inverse`: each subdomain matrix is symmetric positive definite. `coarse_inverse`: each group's matrix is symmetric positive definite. `shared_rows`: own rows of direction d lie in rows d * 256 to (d + 1) * 256 - 1 and are distinct within a list; the own rows of direction 0 of (g, s) are the partner rows of direction 1 of (g, s + 1) and the reverse, likewise directions 2 and 3 between (g, s) and (g + 1, s); entries past the count are rows of the same block. `shared_counts`: the count of direction 0 of (g, s) equals the count of direction 1 of (g, s + 1), that of direction 2 of (g, s) the count of direction 3 of (g + 1, s); counts are 0 where no neighbour exists; some count equals 256.
All inputs are finite; a program needn't handle non-finite values.
Results may differ from a plain program's by a relative error of at most 0.014.
Values may be sent and summed in bfloat16 or wider, within the bound.
A program may use at most 64 MiB of HBM per device.

v0:
```python
import jax
import jax.numpy as jnp
from jax import lax
from jax.sharding import PartitionSpec as P

ITERS = 3


def extended(block, sides, width):
    for axis, dim in sides:
        count = lax.axis_size(axis)
        forward = [(i, i + 1) for i in range(count - 1)]
        backward = [(target, source) for source, target in forward]
        low = lax.ppermute(
            lax.slice_in_dim(block, block.shape[dim] - width, None, axis=dim), axis, forward
        )
        high = lax.ppermute(lax.slice_in_dim(block, 0, width, axis=dim), axis, backward)
        block = jnp.concatenate([low, block, high], axis=dim)
    return block


def pick_rows(tables, indices):
    return jax.vmap(jax.vmap(lambda source_block, rows_at: source_block[rows_at]))(tables, indices)


def add_rows(bases, indices, additions):

    def add_single(base_block, rows_at, extra):
        return base_block.at[rows_at.reshape(-1)].add(extra.reshape(-1, base_block.shape[-1]))

    return jax.vmap(jax.vmap(add_single))(bases, indices, additions)


def count_rows(indices, live_mask, rows_local):

    def count_single(rows_at, mask_rows):
        return (
            jnp.ones((rows_local,), jnp.float32).at[rows_at.reshape(-1)].add(mask_rows.reshape(-1))
        )

    return jax.vmap(jax.vmap(count_single))(indices, live_mask)


def assemble(blocks, own_rows, partner_rows, live_mask):
    padded = extended(blocks, (("group", 0), ("sub", 1)), 1)
    received = jnp.stack(
        [
            pick_rows(padded[1:2, 2:], partner_rows[:, :, 0]),
            pick_rows(padded[1:2, :-2], partner_rows[:, :, 1]),
            pick_rows(padded[2:3, 1:-1], partner_rows[:, :, 2]),
            pick_rows(padded[0:1, 1:-1], partner_rows[:, :, 3]),
        ],
        axis=2,
    )
    values = received * live_mask[..., None]
    return add_rows(blocks, own_rows, values)


def gram_matrix(left, right, weight):
    local_gram = jnp.einsum(
        "gsir,gsic->rc", left * weight[..., None], right, precision=lax.Precision.HIGHEST
    )
    return lax.psum(local_gram, ("group", "sub"))


def spd_solve(matrix, rhs_block):
    factor = jnp.linalg.cholesky(matrix)
    half = lax.linalg.triangular_solve(factor, rhs_block, left_side=True, lower=True)
    return lax.linalg.triangular_solve(factor, half, left_side=True, lower=True, transpose_a=True)


def contract(blocks, mixing):
    return jnp.einsum("gsir,rc->gsic", blocks, mixing, precision=lax.Precision.HIGHEST)


def shards(
    schur, local_inverse, rhs_parts, basis, coarse_map, coarse_inverse, shared_rows, shared_counts
):
    capacity = shared_rows.shape[-1]
    rows_local = rhs_parts.shape[2]
    columns = rhs_parts.shape[3]
    coarse_total = coarse_inverse.shape[2]
    live_mask = (jnp.arange(capacity, dtype=jnp.int32) < shared_counts[..., None]).astype(
        jnp.float32
    )
    own_rows = shared_rows[:, :, 0]
    partner_rows = shared_rows[:, :, 1]
    weight = 1.0 / count_rows(own_rows, live_mask, rows_local)
    selector = (
        coarse_map.reshape(-1)[:, None] == jnp.arange(coarse_total, dtype=jnp.int32)[None, :]
    ).astype(jnp.float32)
    selector_half = selector.astype(jnp.bfloat16)
    full_inverse = coarse_inverse[0]

    def precondition(resid):
        scaled = (weight[..., None] * resid).astype(jnp.bfloat16)
        local_part = jnp.einsum(
            "gsij,gsjr->gsir", local_inverse, scaled, preferred_element_type=jnp.float32
        )
        coarse_local = jnp.einsum(
            "gsmi,gsir->gsmr", basis, scaled, preferred_element_type=jnp.float32
        )
        contrib = jnp.dot(
            selector.T, coarse_local.reshape(-1, columns), precision=lax.Precision.HIGHEST
        )
        coarse_residual = lax.psum(contrib, "sub")
        coarse_rounded = coarse_residual.astype(jnp.bfloat16)
        row_values = jnp.dot(
            full_inverse, coarse_rounded, preferred_element_type=jnp.float32
        ).astype(jnp.bfloat16)
        coarse_values = lax.all_gather(row_values, "sub", axis=0, tiled=True)
        picked = (
            jnp.dot(selector_half, coarse_values, preferred_element_type=jnp.float32)
            .astype(jnp.bfloat16)
            .reshape(coarse_local.shape)
        )
        coarse_part = jnp.einsum(
            "gsmi,gsmr->gsir", basis, picked, preferred_element_type=jnp.float32
        )
        smoothed = weight[..., None] * (local_part + coarse_part)
        return assemble(smoothed, own_rows, partner_rows, live_mask)

    residual = assemble(rhs_parts.astype(jnp.float32), own_rows, partner_rows, live_mask)
    solution = jnp.zeros_like(residual)
    precond = precondition(residual)
    direction = precond
    inner = gram_matrix(precond, residual, weight)
    for iteration in range(ITERS):
        local_image = jnp.einsum(
            "gsij,gsjr->gsir",
            schur,
            direction.astype(jnp.bfloat16),
            preferred_element_type=jnp.float32,
        )
        image = assemble(local_image, own_rows, partner_rows, live_mask)
        curvature = gram_matrix(direction, image, weight)
        step_size = spd_solve(curvature, inner)
        solution = solution + contract(direction, step_size)
        residual = residual - contract(image, step_size)
        if iteration + 1 < ITERS:
            precond = precondition(residual)
            inner_next = gram_matrix(precond, residual, weight)
            conjugacy = spd_solve(inner, inner_next)
            direction = precond + contract(direction, conjugacy)
            inner = inner_next
    return (solution, residual)


def solution(mesh):
    placed = (
        P("group", "sub", None, None),
        P("group", "sub", None, None),
        P("group", "sub", None, None),
        P("group", "sub", None, None),
        P("group", "sub", None),
        P("group", "sub", None),
        P("group", "sub", None, None, None),
        P("group", "sub", None),
    )
    return jax.shard_map(
        shards,
        mesh=mesh,
        in_specs=placed,
        out_specs=(P("group", "sub", None, None), P("group", "sub", None, None)),
        check_vma=False,
    )
```

profile of v0, /device:TPU:1, one launch (start us, length us, event | category | flops | bytes accessed | tf_op | source)
XLA Modules:
  0.0 1686.3 jit_solution(6008829933205526659)
XLA Ops:
  44.1 14.3 collective-permute-done.3
  78.5 66.6 %all-reduce.19 = bf16[1024,128]{1,0:T(8,128)(2,1)} all-reduce(f32[1024,128]{1,0:T(8,128)S(1)} %fusion.81), channel_id=1, replica_groups=mesh['group'=8,'sub'=16] {'sub'}, use_global_device_ids=true, to_apply=%region_2.0 | all-reduce | flops 131072 | bytes 786432 | tf_op jit(solution)/shard_map/psum | solution.py:106
  146.2 18.0 %all_gather.9 = bf16[1024,128]{1,0:T(8,128)(2,1)} all-gather(bf16[64,128]{1,0:T(8,128)(2,1)S(1)} %fusion.21), channel_id=1, replica_groups=mesh['group'=8,'sub'=16] {'sub'}, dimensions={0}, use_global_device_ids=true | all-gather | bytes 278528 | tf_op jit(solution)/shard_map/all_gather | solution.py:111
  165.8 27.7 %collective-permute-start.4 = (f32[1,1,1024,128]{2,3,1,0:T(8,128)S(1)}, f32[1,1,1024,128]{2,3,1,0:T(8,128)S(1)}, u32[]{:S(2)}, u32[]{:S(2)}) collective-permute-start(f32[1,1,1024,128]{2,3,1,0:T(8,128)S(1)} %bitcast.401), channel_id=1, source_target_pairs={{0,16},{16,32},{32,48},{48,64},{64,80},{80,96},{96,112},{1,17},{17... | collective-permute-start | bytes 1572872 | tf_op jit(solution)/shard_map/ppermute | solution.py:14
  222.3 14.5 collective-permute-done.7
  298.6 15.6 collective-permute-done.11
  335.6 149.4 %all-reduce.18.cloned.1.call-done = (f32[128,128]{0,1:T(8,128)}, f32[128,128]{0,1:T(8,128)}) async-done(((f32[128,128]{0,1:T(8,128)}, f32[128,128]{0,1:T(8,128)}), (f32[128,128]{0,1:T(8,128)}, f32[128,128]{0,1:T(8,128)})) %all-reduce.18.cloned.1.call-update) | async-done | bytes 131088 | tf_op jit(solution)/shard_map/psum | solution.py:63
  488.4 12.5 cholesky.89
  502.3 9.8 custom-call.73
  518.9 64.9 %all-reduce.20 = bf16[1024,128]{1,0:T(8,128)(2,1)} all-reduce(f32[1024,128]{1,0:T(8,128)} %fusion.80), channel_id=1, replica_groups=mesh['group'=8,'sub'=16] {'sub'}, use_global_device_ids=true, to_apply=%region_9.13 | all-reduce | flops 131072 | bytes 786432 | tf_op jit(solution)/shard_map/psum | solution.py:106
  584.9 18.3 %all_gather.10 = bf16[1024,128]{1,0:T(8,128)(2,1)} all-gather(bf16[64,128]{1,0:T(8,128)(2,1)S(1)} %fusion.22), channel_id=1, replica_groups=mesh['group'=8,'sub'=16] {'sub'}, dimensions={0}, use_global_device_ids=true | all-gather | bytes 278528 | tf_op jit(solution)/shard_map/all_gather | solution.py:111
  605.6 21.6 %collective-permute-start.12 = (f32[1,1,1024,128]{2,3,1,0:T(8,128)}, f32[1,1,1024,128]{2,3,1,0:T(8,128)S(1)}, u32[]{:S(2)}, u32[]{:S(2)}) collective-permute-start(f32[1,1,1024,128]{2,3,1,0:T(8,128)} %bitcast.405), channel_id=1, source_target_pairs={{0,16},{16,32},{32,48},{48,64},{64,80},{80,96},{96,112},{1,17},{17... | collective-permute-start | bytes 1572872 | tf_op jit(solution)/shard_map/ppermute | solution.py:14
  647.9 12.5 cholesky.100
  699.7 9.8 custom-call.75
  709.5 135.7 %all-reduce.10.cloned.1.call-done = f32[128,128]{0,1:T(8,128)} async-done(((f32[128,128]{0,1:T(8,128)}), f32[128,128]{0,1:T(8,128)}) %all-reduce.10.cloned.1.call-update) | async-done | bytes 65552 | tf_op jit(solution)/shard_map/psum | solution.py:63
  882.4 13.5 collective-permute-done.19
  911.8 8.3 scatter_custom_fusion.5
  923.4 144.1 %all-reduce.12.cloned.1.call-done = f32[128,128]{0,1:T(8,128)} async-done(((f32[128,128]{0,1:T(8,128)}), f32[128,128]{0,1:T(8,128)}) %all-reduce.12.cloned.1.call-update) | async-done | bytes 65552 | tf_op jit(solution)/shard_map/psum | solution.py:63
  1070.6 13.2 cholesky.111
  1087.4 11.3 custom-call.77
  1107.0 64.4 %all-reduce.21 = bf16[1024,128]{1,0:T(8,128)(2,1)} all-reduce(f32[1024,128]{1,0:T(8,128)} %fusion.79), channel_id=1, replica_groups=mesh['group'=8,'sub'=16] {'sub'}, use_global_device_ids=true, to_apply=%region_14.18 | all-reduce | flops 131072 | bytes 786432 | tf_op jit(solution)/shard_map/psum | solution.py:106
  1172.4 18.2 %all_gather.11 = bf16[1024,128]{1,0:T(8,128)(2,1)} all-gather(bf16[64,128]{1,0:T(8,128)(2,1)S(1)} %fusion.23), channel_id=1, replica_groups=mesh['group'=8,'sub'=16] {'sub'}, dimensions={0}, use_global_device_ids=true | all-gather | bytes 278528 | tf_op jit(solution)/shard_map/all_gather | solution.py:111
  1193.0 21.2 %collective-permute-start.20 = (f32[1,1,1024,128]{2,3,1,0:T(8,128)}, f32[1,1,1024,128]{2,3,1,0:T(8,128)S(1)}, u32[]{:S(2)}, u32[]{:S(2)}) collective-permute-start(f32[1,1,1024,128]{2,3,1,0:T(8,128)} %bitcast.397), channel_id=1, source_target_pairs={{0,16},{16,32},{32,48},{48,64},{64,80},{80,96},{96,112},{1,17},{17... | collective-permute-start | bytes 1572872 | tf_op jit(solution)/shard_map/ppermute | solution.py:14
  1233.2 11.7 cholesky.122
  1274.6 8.2 scatter_custom_fusion.6
  1286.7 9.8 custom-call.79
  1296.5 134.3 %all-reduce.14.cloned.1.call-done = f32[128,128]{1,0:T(8,128)} async-done(((f32[128,128]{1,0:T(8,128)}), f32[128,128]{1,0:T(8,128)}) %all-reduce.14.cloned.1.call-update) | async-done | bytes 65552 | tf_op jit(solution)/shard_map/psum | solution.py:63
  1464.9 16.9 %collective-permute-done.27 = f32[3,1,1024,128]{2,3,1,0:T(8,128)} collective-permute-done((f32[3,1,1024,128]{2,3,1,0:T(8,128)}, f32[3,1,1024,128]{2,3,1,0:T(8,128)}, u32[]{:S(2)}, u32[]{:S(2)}) %collective-permute-start.27) | collective-permute-done | bytes 1572896 | tf_op jit(solution)/shard_map/ppermute | solution.py:14
  1494.4 8.5 scatter_custom_fusion.7
  1508.2 142.2 %all-reduce.16.cloned.1.call-done = f32[128,128]{0,1:T(8,128)} async-done(((f32[128,128]{0,1:T(8,128)}), f32[128,128]{0,1:T(8,128)}) %all-reduce.16.cloned.1.call-update) | async-done | bytes 65552 | tf_op jit(solution)/shard_map/psum | solution.py:63
  1652.2 11.7 cholesky.133
  1665.2 9.8 custom-call.81
  (313 shorter events, 432.7 us)
Async XLA Ops:
  7.2 477.8 %all-reduce.18.cloned.1.call-start = ((), (), s32[]{:S(2)}) async-start(), calls=%async_computation.4 | async-start | bytes 262144 | tf_op jit(solution)/shard_map/psum | solution.py:63
  9.2 10.9 collective-permute-start
  13.7 10.8 collective-permute-start.1
  26.9 31.5 %collective-permute-start.3 = (f32[3,1,1024,128]{3,2,1,0:T(8,128)}, f32[3,1,1024,128]{3,2,1,0:T(8,128)}, u32[]{:S(2)}, u32[]{:S(2)}) collective-permute-start(f32[3,1,1024,128]{3,2,1,0:T(8,128)} %pad_maximum_fusion), channel_id=1, source_target_pairs={{0,1},{1,2},{2,3},{3,4},{4,5},{5,6},{6,7},{7,8},{8,9},{9,10},{10,1... | collective-permute-start | bytes 4718600 | tf_op jit(solution)/shard_map/ppermute | solution.py:14
  31.3 32.4 %collective-permute-start.2 = (f32[3,1,1024,128]{3,2,1,0:T(8,128)}, f32[3,1,1024,128]{3,2,1,0:T(8,128)}, u32[]{:S(2)}, u32[]{:S(2)}) collective-permute-start(f32[3,1,1024,128]{3,2,1,0:T(8,128)} %pad_maximum_fusion), channel_id=1, source_target_pairs={{1,0},{2,1},{3,2},{4,3},{5,4},{6,5},{7,6},{8,7},{9,8},{10,9},{11,1... | collective-permute-start | bytes 4718600 | tf_op jit(solution)/shard_map/ppermute | solution.py:17
  165.8 33.9 %collective-permute-start.4 = (f32[1,1,1024,128]{2,3,1,0:T(8,128)S(1)}, f32[1,1,1024,128]{2,3,1,0:T(8,128)S(1)}, u32[]{:S(2)}, u32[]{:S(2)}) collective-permute-start(f32[1,1,1024,128]{2,3,1,0:T(8,128)S(1)} %bitcast.401), channel_id=1, source_target_pairs={{0,16},{16,32},{32,48},{48,64},{64,80},{80,96},{96,112},{1,17},{17... | collective-permute-start | bytes 1572872 | tf_op jit(solution)/shard_map/ppermute | solution.py:14
  193.6 10.5 collective-permute-start.5
  205.4 31.3 %collective-permute-start.7 = (f32[3,1,1024,128]{2,3,1,0:T(8,128)}, f32[3,1,1024,128]{2,3,1,0:T(8,128)}, u32[]{:S(2)}, u32[]{:S(2)}) collective-permute-start(f32[3,1,1024,128]{2,3,1,0:T(8,128)} %pad_maximum_fusion.1), channel_id=1, source_target_pairs={{0,1},{1,2},{2,3},{3,4},{4,5},{5,6},{6,7},{7,8},{8,9},{9,10},{10,1... | collective-permute-start | bytes 4718600 | tf_op jit(solution)/shard_map/ppermute | solution.py:14
  210.0 33.7 %collective-permute-start.6 = (f32[3,1,1024,128]{2,3,1,0:T(8,128)}, f32[3,1,1024,128]{2,3,1,0:T(8,128)}, u32[]{:S(2)}, u32[]{:S(2)}) collective-permute-start(f32[3,1,1024,128]{2,3,1,0:T(8,128)} %pad_maximum_fusion.1), channel_id=1, source_target_pairs={{1,0},{2,1},{3,2},{4,3},{5,4},{6,5},{7,6},{8,7},{9,8},{10,9},{11,1... | collective-permute-start | bytes 4718600 | tf_op jit(solution)/shard_map/ppermute | solution.py:17
  261.9 14.2 collective-permute-start.8
  269.9 10.5 collective-permute-start.9
  281.8 32.4 %collective-permute-start.11 = (f32[3,1,1024,128]{2,3,1,0:T(8,128)}, f32[3,1,1024,128]{2,3,1,0:T(8,128)}, u32[]{:S(2)}, u32[]{:S(2)}) collective-permute-start(f32[3,1,1024,128]{2,3,1,0:T(8,128)} %pad_maximum_fusion.2), channel_id=1, source_target_pairs={{0,1},{1,2},{2,3},{3,4},{4,5},{5,6},{6,7},{7,8},{8,9},{9,10},{10,1... | collective-permute-start | bytes 4718600 | tf_op jit(solution)/shard_map/ppermute | solution.py:14
  287.5 32.0 %collective-permute-start.10 = (f32[3,1,1024,128]{2,3,1,0:T(8,128)}, f32[3,1,1024,128]{2,3,1,0:T(8,128)}, u32[]{:S(2)}, u32[]{:S(2)}) collective-permute-start(f32[3,1,1024,128]{2,3,1,0:T(8,128)} %pad_maximum_fusion.2), channel_id=1, source_target_pairs={{1,0},{2,1},{3,2},{4,3},{5,4},{6,5},{7,6},{8,7},{9,8},{10,9},{11,1... | collective-permute-start | bytes 4718600 | tf_op jit(solution)/shard_map/ppermute | solution.py:17
  335.5 509.6 %all-reduce.10.cloned.1.call-start = ((), (), s32[]{:S(2)}) async-start(), calls=%async_computation | async-start | bytes 131072 | tf_op jit(solution)/shard_map/psum | solution.py:63
  605.6 28.0 %collective-permute-start.12 = (f32[1,1,1024,128]{2,3,1,0:T(8,128)}, f32[1,1,1024,128]{2,3,1,0:T(8,128)S(1)}, u32[]{:S(2)}, u32[]{:S(2)}) collective-permute-start(f32[1,1,1024,128]{2,3,1,0:T(8,128)} %bitcast.405), channel_id=1, source_target_pairs={{0,16},{16,32},{32,48},{48,64},{64,80},{80,96},{96,112},{1,17},{17... | collective-permute-start | bytes 1572872 | tf_op jit(solution)/shard_map/ppermute | solution.py:14
  627.1 10.7 collective-permute-start.13
  640.4 31.3 %collective-permute-start.15 = (f32[3,1,1024,128]{2,3,1,0:T(8,128)}, f32[3,1,1024,128]{2,3,1,0:T(8,128)}, u32[]{:S(2)}, u32[]{:S(2)}) collective-permute-start(f32[3,1,1024,128]{2,3,1,0:T(8,128)} %pad_maximum_fusion.3), channel_id=1, source_target_pairs={{0,1},{1,2},{2,3},{3,4},{4,5},{5,6},{6,7},{7,8},{8,9},{9,10},{10,1... | collective-permute-start | bytes 4718600 | tf_op jit(solution)/shard_map/ppermute | solution.py:14
  644.6 34.0 %collective-permute-start.14 = (f32[3,1,1024,128]{2,3,1,0:T(8,128)}, f32[3,1,1024,128]{2,3,1,0:T(8,128)}, u32[]{:S(2)}, u32[]{:S(2)}) collective-permute-start(f32[3,1,1024,128]{2,3,1,0:T(8,128)} %pad_maximum_fusion.3), channel_id=1, source_target_pairs={{1,0},{2,1},{3,2},{4,3},{5,4},{6,5},{7,6},{8,7},{9,8},{10,9},{11,1... | collective-permute-start | bytes 4718600 | tf_op jit(solution)/shard_map/ppermute | solution.py:17
  698.7 368.8 %all-reduce.12.cloned.1.call-start = ((), (), s32[]{:S(2)}) async-start(), calls=%async_computation.1 | async-start | bytes 131072 | tf_op jit(solution)/shard_map/psum | solution.py:63
  850.5 8.5 collective-permute-start.16
  853.0 10.5 collective-permute-start.17
  864.8 31.1 %collective-permute-start.19 = (f32[3,1,1024,128]{2,3,1,0:T(8,128)}, f32[3,1,1024,128]{2,3,1,0:T(8,128)}, u32[]{:S(2)}, u32[]{:S(2)}) collective-permute-start(f32[3,1,1024,128]{2,3,1,0:T(8,128)} %pad_maximum_fusion.4), channel_id=1, source_target_pairs={{0,1},{1,2},{2,3},{3,4},{4,5},{5,6},{6,7},{7,8},{8,9},{9,10},{10,1... | collective-permute-start | bytes 4718600 | tf_op jit(solution)/shard_map/ppermute | solution.py:14
  868.9 33.9 %collective-permute-start.18 = (f32[3,1,1024,128]{2,3,1,0:T(8,128)}, f32[3,1,1024,128]{2,3,1,0:T(8,128)}, u32[]{:S(2)}, u32[]{:S(2)}) collective-permute-start(f32[3,1,1024,128]{2,3,1,0:T(8,128)} %pad_maximum_fusion.4), channel_id=1, source_target_pairs={{1,0},{2,1},{3,2},{4,3},{5,4},{6,5},{7,6},{8,7},{9,8},{10,9},{11,1... | collective-permute-start | bytes 4718600 | tf_op jit(solution)/shard_map/ppermute | solution.py:17
  922.9 507.9 %all-reduce.14.cloned.1.call-start = ((), (), s32[]{:S(2)}) async-start(), calls=%async_computation.2 | async-start | bytes 131072 | tf_op jit(solution)/shard_map/psum | solution.py:63
  1193.0 27.6 %collective-permute-start.20 = (f32[1,1,1024,128]{2,3,1,0:T(8,128)}, f32[1,1,1024,128]{2,3,1,0:T(8,128)S(1)}, u32[]{:S(2)}, u32[]{:S(2)}) collective-permute-start(f32[1,1,1024,128]{2,3,1,0:T(8,128)} %bitcast.397), channel_id=1, source_target_pairs={{0,16},{16,32},{32,48},{48,64},{64,80},{80,96},{96,112},{1,17},{17... | collective-permute-start | bytes 1572872 | tf_op jit(solution)/shard_map/ppermute | solution.py:14
  1214.2 10.7 collective-permute-start.21
  1227.4 31.3 %collective-permute-start.23 = (f32[3,1,1024,128]{2,3,1,0:T(8,128)}, f32[3,1,1024,128]{2,3,1,0:T(8,128)}, u32[]{:S(2)}, u32[]{:S(2)}) collective-permute-start(f32[3,1,1024,128]{2,3,1,0:T(8,128)} %pad_maximum_fusion.5), channel_id=1, source_target_pairs={{0,1},{1,2},{2,3},{3,4},{4,5},{5,6},{6,7},{7,8},{8,9},{9,10},{10,1... | collective-permute-start | bytes 4718600 | tf_op jit(solution)/shard_map/ppermute | solution.py:14
  1231.6 34.0 %collective-permute-start.22 = (f32[3,1,1024,128]{2,3,1,0:T(8,128)}, f32[3,1,1024,128]{2,3,1,0:T(8,128)}, u32[]{:S(2)}, u32[]{:S(2)}) collective-permute-start(f32[3,1,1024,128]{2,3,1,0:T(8,128)} %pad_maximum_fusion.5), channel_id=1, source_target_pairs={{1,0},{2,1},{3,2},{4,3},{5,4},{6,5},{7,6},{8,7},{9,8},{10,9},{11,1... | collective-permute-start | bytes 4718600 | tf_op jit(solution)/shard_map/ppermute | solution.py:17
  1285.8 364.6 %all-reduce.16.cloned.1.call-start = ((), (), s32[]{:S(2)}) async-start(), calls=%async_computation.3 | async-start | bytes 131072 | tf_op jit(solution)/shard_map/psum | solution.py:63
  1438.9 10.5 collective-permute-start.25
  1450.7 31.1 %collective-permute-start.27 = (f32[3,1,1024,128]{2,3,1,0:T(8,128)}, f32[3,1,1024,128]{2,3,1,0:T(8,128)}, u32[]{:S(2)}, u32[]{:S(2)}) collective-permute-start(f32[3,1,1024,128]{2,3,1,0:T(8,128)} %pad_maximum_fusion.6), channel_id=1, source_target_pairs={{0,1},{1,2},{2,3},{3,4},{4,5},{5,6},{6,7},{7,8},{8,9},{9,10},{10,1... | collective-permute-start | bytes 4718600 | tf_op jit(solution)/shard_map/ppermute | solution.py:14
  1454.9 32.2 %collective-permute-start.26 = (f32[3,1,1024,128]{2,3,1,0:T(8,128)}, f32[3,1,1024,128]{2,3,1,0:T(8,128)}, u32[]{:S(2)}, u32[]{:S(2)}) collective-permute-start(f32[3,1,1024,128]{2,3,1,0:T(8,128)} %pad_maximum_fusion.6), channel_id=1, source_target_pairs={{1,0},{2,1},{3,2},{4,3},{5,4},{6,5},{7,6},{8,7},{9,8},{10,9},{11,1... | collective-permute-start | bytes 4718600 | tf_op jit(solution)/shard_map/ppermute | solution.py:17
  (35 other events, 1593.9 us)
Sparse Core Ops, SparseCore 0:
  335.7 149.2 all-reduce.17
  698.8 146.3 all-reduce.9
  923.0 144.4 all-reduce.11
  1285.9 144.8 all-reduce.13
  1505.9 144.4 all-reduce.15
where the time goes:
time: 1700 us; the launch traced here: 1690 us
  waiting for transfers between devices  842 us (50%)
  blocking collectives  250 us (15%)
  other arithmetic  218 us (13%)
  local copies, waits for them, and re-layouts  155 us (9%)
  starting transfers between devices  143 us (8%)
  matrix products  63.4 us (4%)
    psum x5, waiting for transfers between devices, gram_matrix(): return lax.psum(local_gram, ('group', 'sub'))  706 us
    psum x3, blocking collectives, precondition(): coarse_residual = lax.psum(contrib, 'sub')  196 us
    ppermute x14, starting transfers between devices, extended(): lax.ppermute(lax.slice_in_dim(block, block.shape[dim] - width, None, axis...  119 us
    ppermute x14, waiting for transfers between devices, extended(): lax.ppermute(lax.slice_in_dim(block, block.shape[dim] - width, None, axis...  103 us
    gather x28, local copies, waits for them, and re-layouts, pick_rows(): source_block[rows_at]  70.6 us
    another operation x15, other arithmetic, spd_solve(): factor = jnp.linalg.cholesky(matrix)  66 us
    another operation x10, other arithmetic, spd_solve(): lax.linalg.triangular_solve(factor, half, left_side=True, lower=True, tra...  55.3 us
    all_gather x3, blocking collectives, precondition(): coarse_values = lax.all_gather(row_values, 'sub', axis=0, tiled=True)  54.4 us
  transfers between devices with their start and end apart: 33, of which 27 were waited for; matrix products, arithmetic and copies ran while one was open for 10% of the time, Pallas kernels for 0%

commit v1 on v0

--- a/solution.py
+++ b/solution.py
@@ -4,6 +4,12 @@
 from jax.sharding import PartitionSpec as P
 
 ITERS = 3
+
+
+def summed_here(array, name):
+    parts = lax.all_gather(array, name, axis=0, tiled=False)
+    total = parts.sum(axis=0)
+    return total
 
 
 def extended(block, sides, width):
@@ -60,7 +66,7 @@
     local_gram = jnp.einsum(
         "gsir,gsic->rc", left * weight[..., None], right, precision=lax.Precision.HIGHEST
     )
-    return lax.psum(local_gram, ("group", "sub"))
+    return summed_here(local_gram, ("group", "sub"))
 
 
 def spd_solve(matrix, rhs_block):

time: 1700 us -> 1380 us (0.81)
  waiting for transfers between devices: 842 us -> 503 us
    psum x5 -> x0, waiting for transfers between devices: 706 us -> none  [gram_matrix(): return lax.psum(local_gram, ('group', 'sub'))]
    all_gather x0 -> x6, waiting for transfers between devices: none -> 348 us  [summed_here(): parts = lax.all_gather(array, name, axis=0, tiled=False)]
    reduce_sum x0 -> x6, other arithmetic: none -> 22.9 us  [summed_here(): total = parts.sum(axis=0)]
    ppermute x14, waiting for transfers between devices: 103 us -> 122 us  [extended(): lax.ppermute(lax.slice_in_dim(block, block.shape[dim] - width, None, axis...]
  transfers between devices with their start and end apart: 33 -> 34, of which waited for: 27 -> 28; matrix products, arithmetic and copies ran while one was open for 10% -> 15% of each run, Pallas kernels for 0% -> 0%
where the time goes in v1:
time: 1380 us; the launch traced here: 1370 us
  waiting for transfers between devices  503 us (36%)
  blocking collectives  250 us (18%)
  other arithmetic  234 us (17%)
  local copies, waits for them, and re-layouts  167 us (12%)
  starting transfers between devices  142 us (10%)
  matrix products  58.3 us (4%)
  between operations  15.6 us (1%)
    all_gather x6, waiting for transfers between devices, summed_here(): parts = lax.all_gather(array, name, axis=0, tiled=False)  348 us
    psum x3, blocking collectives, precondition(): coarse_residual = lax.psum(contrib, 'sub')  196 us
    ppermute x14, waiting for transfers between devices, extended(): lax.ppermute(lax.slice_in_dim(block, block.shape[dim] - width, None, axis...  122 us
    ppermute x14, starting transfers between devices, extended(): lax.ppermute(lax.slice_in_dim(block, block.shape[dim] - width, None, axis...  117 us
    gather x28, local copies, waits for them, and re-layouts, pick_rows(): source_block[rows_at]  79.1 us
    another operation x15, other arithmetic, spd_solve(): factor = jnp.linalg.cholesky(matrix)  62.9 us
    all_gather x3, blocking collectives, precondition(): coarse_values = lax.all_gather(row_values, 'sub', axis=0, tiled=True)  54.5 us
    another operation x10, other arithmetic, spd_solve(): lax.linalg.triangular_solve(factor, half, left_side=True, lower=True, tra...  53.8 us
  transfers between devices with their start and end apart: 34, of which 28 were waited for; matrix products, arithmetic and copies ran while one was open for 15% of the time, Pallas kernels for 0%

profile of v1, /device:TPU:1, one launch (start us, length us, event | category | flops | bytes accessed | tf_op | source)
XLA Modules:
  0.0 1371.2 jit_solution(5008210219202996138)
XLA Ops:
  44.1 14.4 %collective-permute-done.3 = f32[3,1,1024,128]{3,2,1,0:T(8,128)} collective-permute-done((f32[3,1,1024,128]{3,2,1,0:T(8,128)}, f32[3,1,1024,128]{3,2,1,0:T(8,128)}, u32[]{:S(2)}, u32[]{:S(2)}) %collective-permute-start.3) | collective-permute-done | bytes 1572896 | tf_op jit(solution)/shard_map/ppermute | solution.py:20
  78.4 66.6 %all-reduce.3 = bf16[1024,128]{1,0:T(8,128)(2,1)} all-reduce(f32[1024,128]{1,0:T(8,128)S(1)} %fusion.81), channel_id=1, replica_groups=mesh['group'=8,'sub'=16] {'sub'}, use_global_device_ids=true, to_apply=%region_2.0 | all-reduce | flops 131072 | bytes 786432 | tf_op jit(solution)/shard_map/psum | solution.py:112
  146.2 18.0 %all_gather.45 = bf16[1024,128]{1,0:T(8,128)(2,1)} all-gather(bf16[64,128]{1,0:T(8,128)(2,1)S(1)} %fusion.21), channel_id=1, replica_groups=mesh['group'=8,'sub'=16] {'sub'}, dimensions={0}, use_global_device_ids=true | all-gather | bytes 278528 | tf_op jit(solution)/shard_map/all_gather | solution.py:117
  165.8 27.8 %collective-permute-start.4 = (f32[1,1,1024,128]{2,3,1,0:T(8,128)S(1)}, f32[1,1,1024,128]{2,3,1,0:T(8,128)S(1)}, u32[]{:S(2)}, u32[]{:S(2)}) collective-permute-start(f32[1,1,1024,128]{2,3,1,0:T(8,128)S(1)} %bitcast.409), channel_id=1, source_target_pairs={{0,16},{16,32},{32,48},{48,64},{64,80},{80,96},{96,112},{1,17},{17... | collective-permute-start | bytes 1572872 | tf_op jit(solution)/shard_map/ppermute | solution.py:20
  222.9 13.8 %collective-permute-done.7 = f32[3,1,1024,128]{2,3,1,0:T(8,128)} collective-permute-done((f32[3,1,1024,128]{2,3,1,0:T(8,128)}, f32[3,1,1024,128]{2,3,1,0:T(8,128)}, u32[]{:S(2)}, u32[]{:S(2)}) %collective-permute-start.7) | collective-permute-done | bytes 1572896 | tf_op jit(solution)/shard_map/ppermute | solution.py:20
  302.5 14.0 %collective-permute-done.11 = f32[3,1,1024,128]{2,3,1,0:T(8,128)} collective-permute-done((f32[3,1,1024,128]{2,3,1,0:T(8,128)}, f32[3,1,1024,128]{2,3,1,0:T(8,128)}, u32[]{:S(2)}, u32[]{:S(2)}) %collective-permute-start.11) | collective-permute-done | bytes 1572896 | tf_op jit(solution)/shard_map/ppermute | solution.py:20
  341.5 24.0 %all-gather.15.cloned.1.call-done = f32[16384,128]{1,0:T(8,128)} async-done(((f32[128,128]{1,0:T(8,128)}), f32[16384,128]{1,0:T(8,128)}) %all-gather.15.cloned.1.call-update) | async-done | bytes 8388624 | tf_op jit(solution)/shard_map/all_gather | solution.py:10
  369.4 67.1 %all-gather.13.cloned.1.call-done = f32[16384,128]{1,0:T(8,128)} async-done(((f32[128,128]{1,0:T(8,128)}), f32[16384,128]{1,0:T(8,128)}) %all-gather.13.cloned.1.call-update) | async-done | bytes 8388624 | tf_op jit(solution)/shard_map/all_gather | solution.py:10
  440.4 11.7 cholesky.89
  453.5 9.8 custom-call.73
  469.8 64.3 %all-reduce.4 = bf16[1024,128]{1,0:T(8,128)(2,1)} all-reduce(f32[1024,128]{1,0:T(8,128)} %fusion.80), channel_id=1, replica_groups=mesh['group'=8,'sub'=16] {'sub'}, use_global_device_ids=true, to_apply=%region_9.13 | all-reduce | flops 131072 | bytes 786432 | tf_op jit(solution)/shard_map/psum | solution.py:112
  535.3 18.1 %all_gather.50 = bf16[1024,128]{1,0:T(8,128)(2,1)} all-gather(bf16[64,128]{1,0:T(8,128)(2,1)S(1)} %fusion.22), channel_id=1, replica_groups=mesh['group'=8,'sub'=16] {'sub'}, dimensions={0}, use_global_device_ids=true | all-gather | bytes 278528 | tf_op jit(solution)/shard_map/all_gather | solution.py:117
  555.8 21.3 %collective-permute-start.12 = (f32[1,1,1024,128]{2,3,1,0:T(8,128)}, f32[1,1,1024,128]{2,3,1,0:T(8,128)S(1)}, u32[]{:S(2)}, u32[]{:S(2)}) collective-permute-start(f32[1,1,1024,128]{2,3,1,0:T(8,128)} %bitcast.413), channel_id=1, source_target_pairs={{0,16},{16,32},{32,48},{48,64},{64,80},{80,96},{96,112},{1,17},{17... | collective-permute-start | bytes 1572872 | tf_op jit(solution)/shard_map/ppermute | solution.py:20
  608.2 13.5 collective-permute-done.15
  649.1 11.7 cholesky.100
  662.2 9.8 custom-call.75
  672.0 53.4 %all-gather.17.cloned.1.call-done = f32[16384,128]{1,0:T(8,128)} async-done(((f32[128,128]{1,0:T(8,128)}), f32[16384,128]{1,0:T(8,128)}) %all-gather.17.cloned.1.call-update) | async-done | bytes 8388624 | tf_op jit(solution)/shard_map/all_gather | solution.py:10
  765.1 13.0 collective-permute-done.19
  805.6 75.9 %all-gather.19.cloned.1.call-done = f32[16384,128]{1,0:T(8,128)} async-done(((f32[128,128]{1,0:T(8,128)}), f32[16384,128]{1,0:T(8,128)}) %all-gather.19.cloned.1.call-update) | async-done | bytes 8388624 | tf_op jit(solution)/shard_map/all_gather | solution.py:10
  887.5 12.5 cholesky.111
  902.1 10.6 custom-call.77
  920.2 64.6 %all-reduce.5 = bf16[1024,128]{1,0:T(8,128)(2,1)} all-reduce(f32[1024,128]{1,0:T(8,128)} %fusion.79), channel_id=1, replica_groups=mesh['group'=8,'sub'=16] {'sub'}, use_global_device_ids=true, to_apply=%region_14.18 | all-reduce | flops 131072 | bytes 786432 | tf_op jit(solution)/shard_map/psum | solution.py:112
  985.9 18.4 %all_gather.55 = bf16[1024,128]{1,0:T(8,128)(2,1)} all-gather(bf16[64,128]{1,0:T(8,128)(2,1)S(1)} %fusion.23), channel_id=1, replica_groups=mesh['group'=8,'sub'=16] {'sub'}, dimensions={0}, use_global_device_ids=true | all-gather | bytes 278528 | tf_op jit(solution)/shard_map/all_gather | solution.py:117
  1006.7 20.8 %collective-permute-start.20 = (f32[1,1,1024,128]{2,3,1,0:T(8,128)}, f32[1,1,1024,128]{2,3,1,0:T(8,128)S(1)}, u32[]{:S(2)}, u32[]{:S(2)}) collective-permute-start(f32[1,1,1024,128]{2,3,1,0:T(8,128)} %bitcast.417), channel_id=1, source_target_pairs={{0,16},{16,32},{32,48},{48,64},{64,80},{80,96},{96,112},{1,17},{17... | collective-permute-start | bytes 1572872 | tf_op jit(solution)/shard_map/ppermute | solution.py:20
  1058.0 14.1 %collective-permute-done.23 = f32[3,1,1024,128]{2,3,1,0:T(8,128)} collective-permute-done((f32[3,1,1024,128]{2,3,1,0:T(8,128)}, f32[3,1,1024,128]{2,3,1,0:T(8,128)}, u32[]{:S(2)}, u32[]{:S(2)}) %collective-permute-start.23) | collective-permute-done | bytes 1572896 | tf_op jit(solution)/shard_map/ppermute | solution.py:20
  1099.5 11.7 cholesky.122
  1112.6 9.8 custom-call.79
  1122.4 53.3 %all-gather.21.cloned.1.call-done = f32[16384,128]{1,0:T(8,128)} async-done(((f32[128,128]{1,0:T(8,128)}), f32[16384,128]{1,0:T(8,128)}) %all-gather.21.cloned.1.call-update) | async-done | bytes 8388624 | tf_op jit(solution)/shard_map/all_gather | solution.py:10
  1215.2 13.6 collective-permute-done.27
  1258.1 74.5 %all-gather.23.cloned.1.call-done = f32[16384,128]{1,0:T(8,128)} async-done(((f32[128,128]{1,0:T(8,128)}), f32[16384,128]{1,0:T(8,128)}) %all-gather.23.cloned.1.call-update) | async-done | bytes 8388624 | tf_op jit(solution)/shard_map/all_gather | solution.py:10
  1336.6 11.7 cholesky.133
  1349.8 9.8 custom-call.81
  (317 shorter events, 481.8 us)
Async XLA Ops:
  7.2 358.4 %all-gather.15.cloned.1.call-start = ((), (), s32[]{:S(2)}) async-start(), calls=%async_computation.1 | async-start | bytes 8454144 | tf_op jit(solution)/shard_map/all_gather | solution.py:10
  9.2 10.9 collective-permute-start
  13.7 10.8 collective-permute-start.1
  26.9 31.5 %collective-permute-start.3 = (f32[3,1,1024,128]{3,2,1,0:T(8,128)}, f32[3,1,1024,128]{3,2,1,0:T(8,128)}, u32[]{:S(2)}, u32[]{:S(2)}) collective-permute-start(f32[3,1,1024,128]{3,2,1,0:T(8,128)} %pad_maximum_fusion), channel_id=1, source_target_pairs={{0,1},{1,2},{2,3},{3,4},{4,5},{5,6},{6,7},{7,8},{8,9},{9,10},{10,1... | collective-permute-start | bytes 4718600 | tf_op jit(solution)/shard_map/ppermute | solution.py:20
  31.3 32.4 %collective-permute-start.2 = (f32[3,1,1024,128]{3,2,1,0:T(8,128)}, f32[3,1,1024,128]{3,2,1,0:T(8,128)}, u32[]{:S(2)}, u32[]{:S(2)}) collective-permute-start(f32[3,1,1024,128]{3,2,1,0:T(8,128)} %pad_maximum_fusion), channel_id=1, source_target_pairs={{1,0},{2,1},{3,2},{4,3},{5,4},{6,5},{7,6},{8,7},{9,8},{10,9},{11,1... | collective-permute-start | bytes 4718600 | tf_op jit(solution)/shard_map/ppermute | solution.py:23
  165.8 33.9 %collective-permute-start.4 = (f32[1,1,1024,128]{2,3,1,0:T(8,128)S(1)}, f32[1,1,1024,128]{2,3,1,0:T(8,128)S(1)}, u32[]{:S(2)}, u32[]{:S(2)}) collective-permute-start(f32[1,1,1024,128]{2,3,1,0:T(8,128)S(1)} %bitcast.409), channel_id=1, source_target_pairs={{0,16},{16,32},{32,48},{48,64},{64,80},{80,96},{96,112},{1,17},{17... | collective-permute-start | bytes 1572872 | tf_op jit(solution)/shard_map/ppermute | solution.py:20
  193.5 10.5 collective-permute-start.5
  205.4 31.3 %collective-permute-start.7 = (f32[3,1,1024,128]{2,3,1,0:T(8,128)}, f32[3,1,1024,128]{2,3,1,0:T(8,128)}, u32[]{:S(2)}, u32[]{:S(2)}) collective-permute-start(f32[3,1,1024,128]{2,3,1,0:T(8,128)} %pad_maximum_fusion.1), channel_id=1, source_target_pairs={{0,1},{1,2},{2,3},{3,4},{4,5},{5,6},{6,7},{7,8},{8,9},{9,10},{10,1... | collective-permute-start | bytes 4718600 | tf_op jit(solution)/shard_map/ppermute | solution.py:20
  209.9 33.7 %collective-permute-start.6 = (f32[3,1,1024,128]{2,3,1,0:T(8,128)}, f32[3,1,1024,128]{2,3,1,0:T(8,128)}, u32[]{:S(2)}, u32[]{:S(2)}) collective-permute-start(f32[3,1,1024,128]{2,3,1,0:T(8,128)} %pad_maximum_fusion.1), channel_id=1, source_target_pairs={{1,0},{2,1},{3,2},{4,3},{5,4},{6,5},{7,6},{8,7},{9,8},{10,9},{11,1... | collective-permute-start | bytes 4718600 | tf_op jit(solution)/shard_map/ppermute | solution.py:23
  261.3 175.2 %all-gather.13.cloned.1.call-start = ((), (), s32[]{:S(2)}) async-start(), calls=%async_computation | async-start | bytes 8454144 | tf_op jit(solution)/shard_map/all_gather | solution.py:10
  263.7 14.3 %collective-permute-start.8 = (f32[1,1,1024,128]{2,3,1,0:T(8,128)S(1)}, f32[1,1,1024,128]{2,3,1,0:T(8,128)S(1)}, u32[]{:S(2)}, u32[]{:S(2)}) collective-permute-start(f32[1,1,1024,128]{2,3,1,0:T(8,128)S(1)} %bitcast.421), channel_id=1, source_target_pairs={{0,16},{16,32},{32,48},{48,64},{64,80},{80,96},{96,112},{1,17},{17... | collective-permute-start | bytes 1572872 | tf_op jit(solution)/shard_map/ppermute | solution.py:20
  271.8 10.8 collective-permute-start.9
  284.0 32.5 %collective-permute-start.11 = (f32[3,1,1024,128]{2,3,1,0:T(8,128)}, f32[3,1,1024,128]{2,3,1,0:T(8,128)}, u32[]{:S(2)}, u32[]{:S(2)}) collective-permute-start(f32[3,1,1024,128]{2,3,1,0:T(8,128)} %pad_maximum_fusion.2), channel_id=1, source_target_pairs={{0,1},{1,2},{2,3},{3,4},{4,5},{5,6},{6,7},{7,8},{8,9},{9,10},{10,1... | collective-permute-start | bytes 4718600 | tf_op jit(solution)/shard_map/ppermute | solution.py:20
  289.8 33.6 %collective-permute-start.10 = (f32[3,1,1024,128]{2,3,1,0:T(8,128)}, f32[3,1,1024,128]{2,3,1,0:T(8,128)}, u32[]{:S(2)}, u32[]{:S(2)}) collective-permute-start(f32[3,1,1024,128]{2,3,1,0:T(8,128)} %pad_maximum_fusion.2), channel_id=1, source_target_pairs={{1,0},{2,1},{3,2},{4,3},{5,4},{6,5},{7,6},{8,7},{9,8},{10,9},{11,1... | collective-permute-start | bytes 4718600 | tf_op jit(solution)/shard_map/ppermute | solution.py:23
  341.5 383.9 %all-gather.17.cloned.1.call-start = ((), (), s32[]{:S(2)}) async-start(), calls=%async_computation.2 | async-start | bytes 8454144 | tf_op jit(solution)/shard_map/all_gather | solution.py:10
  555.8 27.8 %collective-permute-start.12 = (f32[1,1,1024,128]{2,3,1,0:T(8,128)}, f32[1,1,1024,128]{2,3,1,0:T(8,128)S(1)}, u32[]{:S(2)}, u32[]{:S(2)}) collective-permute-start(f32[1,1,1024,128]{2,3,1,0:T(8,128)} %bitcast.413), channel_id=1, source_target_pairs={{0,16},{16,32},{32,48},{48,64},{64,80},{80,96},{96,112},{1,17},{17... | collective-permute-start | bytes 1572872 | tf_op jit(solution)/shard_map/ppermute | solution.py:20
  577.2 10.7 collective-permute-start.13
  590.4 31.3 %collective-permute-start.15 = (f32[3,1,1024,128]{2,3,1,0:T(8,128)}, f32[3,1,1024,128]{2,3,1,0:T(8,128)}, u32[]{:S(2)}, u32[]{:S(2)}) collective-permute-start(f32[3,1,1024,128]{2,3,1,0:T(8,128)} %pad_maximum_fusion.3), channel_id=1, source_target_pairs={{0,1},{1,2},{2,3},{3,4},{4,5},{5,6},{6,7},{7,8},{8,9},{9,10},{10,1... | collective-permute-start | bytes 4718600 | tf_op jit(solution)/shard_map/ppermute | solution.py:20
  594.6 34.0 %collective-permute-start.14 = (f32[3,1,1024,128]{2,3,1,0:T(8,128)}, f32[3,1,1024,128]{2,3,1,0:T(8,128)}, u32[]{:S(2)}, u32[]{:S(2)}) collective-permute-start(f32[3,1,1024,128]{2,3,1,0:T(8,128)} %pad_maximum_fusion.3), channel_id=1, source_target_pairs={{1,0},{2,1},{3,2},{4,3},{5,4},{6,5},{7,6},{8,7},{9,8},{10,9},{11,1... | collective-permute-start | bytes 4718600 | tf_op jit(solution)/shard_map/ppermute | solution.py:23
  648.7 232.8 %all-gather.19.cloned.1.call-start = ((), (), s32[]{:S(2)}) async-start(), calls=%async_computation.3 | async-start | bytes 8454144 | tf_op jit(solution)/shard_map/all_gather | solution.py:10
  735.8 10.5 collective-permute-start.17
  747.6 30.5 %collective-permute-start.19 = (f32[3,1,1024,128]{2,3,1,0:T(8,128)}, f32[3,1,1024,128]{2,3,1,0:T(8,128)}, u32[]{:S(2)}, u32[]{:S(2)}) collective-permute-start(f32[3,1,1024,128]{2,3,1,0:T(8,128)} %pad_maximum_fusion.4), channel_id=1, source_target_pairs={{0,1},{1,2},{2,3},{3,4},{4,5},{5,6},{6,7},{7,8},{8,9},{9,10},{10,1... | collective-permute-start | bytes 4718600 | tf_op jit(solution)/shard_map/ppermute | solution.py:20
  751.4 33.7 %collective-permute-start.18 = (f32[3,1,1024,128]{2,3,1,0:T(8,128)}, f32[3,1,1024,128]{2,3,1,0:T(8,128)}, u32[]{:S(2)}, u32[]{:S(2)}) collective-permute-start(f32[3,1,1024,128]{2,3,1,0:T(8,128)} %pad_maximum_fusion.4), channel_id=1, source_target_pairs={{1,0},{2,1},{3,2},{4,3},{5,4},{6,5},{7,6},{8,7},{9,8},{10,9},{11,1... | collective-permute-start | bytes 4718600 | tf_op jit(solution)/shard_map/ppermute | solution.py:23
  805.1 370.6 %all-gather.21.cloned.1.call-start = ((), (), s32[]{:S(2)}) async-start(), calls=%async_computation.4 | async-start | bytes 8454144 | tf_op jit(solution)/shard_map/all_gather | solution.py:10
  1006.7 27.2 %collective-permute-start.20 = (f32[1,1,1024,128]{2,3,1,0:T(8,128)}, f32[1,1,1024,128]{2,3,1,0:T(8,128)S(1)}, u32[]{:S(2)}, u32[]{:S(2)}) collective-permute-start(f32[1,1,1024,128]{2,3,1,0:T(8,128)} %bitcast.417), channel_id=1, source_target_pairs={{0,16},{16,32},{32,48},{48,64},{64,80},{80,96},{96,112},{1,17},{17... | collective-permute-start | bytes 1572872 | tf_op jit(solution)/shard_map/ppermute | solution.py:20
  1027.5 10.7 collective-permute-start.21
  1040.7 31.3 %collective-permute-start.23 = (f32[3,1,1024,128]{2,3,1,0:T(8,128)}, f32[3,1,1024,128]{2,3,1,0:T(8,128)}, u32[]{:S(2)}, u32[]{:S(2)}) collective-permute-start(f32[3,1,1024,128]{2,3,1,0:T(8,128)} %pad_maximum_fusion.5), channel_id=1, source_target_pairs={{0,1},{1,2},{2,3},{3,4},{4,5},{5,6},{6,7},{7,8},{8,9},{9,10},{10,1... | collective-permute-start | bytes 4718600 | tf_op jit(solution)/shard_map/ppermute | solution.py:20
  1044.9 34.0 %collective-permute-start.22 = (f32[3,1,1024,128]{2,3,1,0:T(8,128)}, f32[3,1,1024,128]{2,3,1,0:T(8,128)}, u32[]{:S(2)}, u32[]{:S(2)}) collective-permute-start(f32[3,1,1024,128]{2,3,1,0:T(8,128)} %pad_maximum_fusion.5), channel_id=1, source_target_pairs={{1,0},{2,1},{3,2},{4,3},{5,4},{6,5},{7,6},{8,7},{9,8},{10,9},{11,1... | collective-permute-start | bytes 4718600 | tf_op jit(solution)/shard_map/ppermute | solution.py:23
  1099.2 233.4 %all-gather.23.cloned.1.call-start = ((), (), s32[]{:S(2)}) async-start(), calls=%async_computation.5 | async-start | bytes 8454144 | tf_op jit(solution)/shard_map/all_gather | solution.py:10
  1186.4 10.5 collective-permute-start.25
  1198.2 30.5 %collective-permute-start.27 = (f32[3,1,1024,128]{2,3,1,0:T(8,128)}, f32[3,1,1024,128]{2,3,1,0:T(8,128)}, u32[]{:S(2)}, u32[]{:S(2)}) collective-permute-start(f32[3,1,1024,128]{2,3,1,0:T(8,128)} %pad_maximum_fusion.6), channel_id=1, source_target_pairs={{0,1},{1,2},{2,3},{3,4},{4,5},{5,6},{6,7},{7,8},{8,9},{9,10},{10,1... | collective-permute-start | bytes 4718600 | tf_op jit(solution)/shard_map/ppermute | solution.py:20
  1202.0 33.7 %collective-permute-start.26 = (f32[3,1,1024,128]{2,3,1,0:T(8,128)}, f32[3,1,1024,128]{2,3,1,0:T(8,128)}, u32[]{:S(2)}, u32[]{:S(2)}) collective-permute-start(f32[3,1,1024,128]{2,3,1,0:T(8,128)} %pad_maximum_fusion.6), channel_id=1, source_target_pairs={{1,0},{2,1},{3,2},{4,3},{5,4},{6,5},{7,6},{8,7},{9,8},{10,9},{11,1... | collective-permute-start | bytes 4718600 | tf_op jit(solution)/shard_map/ppermute | solution.py:23
  (33 other events, 771.4 us)
Sparse Core Ops, SparseCore 0:
  261.4 104.1 all-gather.14
  369.3 67.1 all-gather.12
  648.8 76.5 all-gather.16
  805.3 76.2 all-gather.18
  1099.3 76.4 all-gather.20
  1256.3 76.2 all-gather.22
